TPU v7x, 32 devices: a whole 2x2x4 slice. The times are simulated.
32 devices in a mesh: groups: 2 (over x), tensor: 16 (over z, y, core).
Axes of the slice: x: 2, y: 2, z: 4, core: 2. Of those that a mesh axis runs over, the one named last changes fastest.
Arguments:
- tokens: bfloat16 [1024, 8192], P('groups', 'tensor'), parts along dimension 0, may hold values from -6 to 6
- norm_gain: float32 [8192], P('tensor'), may hold values from 0.1 to 1.9
- w_in: bfloat16 [8192, 3, 8192], P(None, None, 'tensor'), may hold values from -0.0625 to 0.0625
- w_short: float32 [3, 3, 8192], P(None, None, 'tensor'), may hold values from -3 to 3
- filters: bfloat16 [512, 128], P('tensor'), may hold values from -0.5 to 0.5
- skip: float32 [8192], P('tensor'), may hold values from -4 to 4
- w_out: bfloat16 [8192, 8192], P('tensor'), may hold values from -0.0625 to 0.0625
Outputs:
- mixed: bfloat16 [1024, 8192], P('groups', 'tensor'), parts along dimension 0
There are 2 independent parts, one for each index of `groups`. A program takes and returns all parts, laid end to end along the dimension named above; an argument that names none is the same for every part. Nothing has to cross between parts.
All inputs are finite; a program needn't handle non-finite values.
Results may differ from a plain program's by a relative error of at most 0.0085.
Values may be sent and summed in bfloat16 or wider, within the bound.
A program may use at most 192 MiB of HBM per device.

v0:
```python
import jax
import jax.numpy as jnp
from jax import lax
from jax.sharding import PartitionSpec as P

D = 8192


def shifted(field, lag):
    pads = ((lag, 0),) + ((0, 0),) * (field.ndim - 1)
    return jnp.pad(field, pads)[: field.shape[0]]


def lag_matrix(filters, rows):
    count, taps = filters.shape
    length = taps + rows
    line = jnp.concatenate([filters, jnp.zeros((count, rows), filters.dtype)], axis=1)
    tiled = jnp.tile(line, (1, rows))[:, : rows * (length - 1)]
    return tiled.reshape(count, rows, length - 1)[:, :, :rows]


def on_device(tokens, norm_gain, w_in, w_short, filters, skip, w_out):
    wide = tokens.astype(jnp.float32)
    squares = lax.psum(jnp.sum(wide * wide, axis=1, keepdims=True), "tensor")
    factor = lax.rsqrt(squares / D + 1e-05)
    normed = (wide * factor * norm_gain[None, :]).astype(jnp.bfloat16)
    width = w_in.shape[0]
    local = w_in.shape[2]
    rows = tokens.shape[0]
    w_flat = w_in.reshape(width, 3 * local)
    chosen = w_flat
    proj = jnp.dot(
        lax.all_gather(normed, "tensor", axis=1, tiled=True),
        chosen,
        preferred_element_type=jnp.float32,
    )
    proj = proj.reshape(rows, 3, local)
    short = w_short[0][None] * proj
    for lag in range(1, w_short.shape[0]):
        short = short + w_short[lag][None] * shifted(proj, lag)
    gated = (short[:, 1] * short[:, 2]).astype(jnp.bfloat16)
    count = filters.shape[0]
    lagged = lag_matrix(filters, rows)
    grouped = gated.reshape(rows, count, local // count)
    conv = jnp.einsum("fst,sfg->tfg", lagged, grouped, preferred_element_type=jnp.float32)
    conv = conv.reshape(rows, local)
    hidden = ((conv + skip[None, :] * gated.astype(jnp.float32)) * short[:, 0]).astype(jnp.bfloat16)
    w_cols = lax.all_to_all(w_out, "tensor", split_axis=1, concat_axis=0, tiled=True)
    chosen = w_cols
    summed = jnp.dot(
        lax.all_gather(hidden, "tensor", axis=1, tiled=True),
        chosen,
        preferred_element_type=jnp.float32,
    )
    return (wide + summed).astype(jnp.bfloat16)


def solution(mesh):
    return jax.shard_map(
        on_device,
        mesh=mesh,
        in_specs=(
            P("groups", "tensor"),
            P("tensor"),
            P(None, None, "tensor"),
            P(None, None, "tensor"),
            P("tensor", None),
            P("tensor"),
            P("tensor", None),
        ),
        out_specs=P("groups", "tensor"),
        check_vma=False,
    )
```

profile of v0, /device:TPU:0, one launch (start us, length us, event | category | flops | bytes accessed | tf_op | source)
XLA Modules:
  0.0 382.3 jit_solution(3870038537014596827)
XLA Ops:
  6.5 0.0 all-gather.3.cloned.1.call-start
  6.5 1.2 fusion.10
  7.8 35.0 %psum.7 = f32[512,1]{0,1:T(1,128)S(1)} all-reduce(f32[512,1]{0,1:T(1,128)S(1)} %bitcast.46), channel_id=1, replica_groups=mesh['groups'=2,'tensor'=16] {'tensor'}, use_global_device_ids=true, to_apply=%region_1.0 | all-reduce | flops 512 | bytes 4096 | tf_op jit(solution)/shard_map/psum | solution.py:24
  42.7 2.0 fusion.12
  44.7 0.0 all-gather.3.cloned.1.call-update
  44.8 12.1 %copy.16 = bf16[512,8192]{0,1:T(8,128)(2,1)} copy(bf16[512,8192]{1,0:T(8,128)(2,1)} %param.13) | data formatting | bytes 16777216 | tf_op args[6]
  56.8 4.8 %all-to-all-start = ((bf16[512,16,512]{0,2,1:T(8,128)(2,1)}), bf16[512,16,512]{0,2,1:T(8,128)(2,1)}, u32[]{:S(2)}, u32[]{:S(2)}) async-start(bf16[512,16,512]{0,2,1:T(8,128)(2,1)} %bitcast.41), calls=%async_computation | async-start | bytes 16777216 | tf_op jit(solution)/shard_map/all_to_all | solution.py:48
  61.6 0.0 copy-start.2
  61.6 0.0 all-gather.5.cloned.1.call-start
  61.7 33.5 %copy.13 = bf16[8192,3,512]{0,2,1:T(8,128)(2,1)} copy(bf16[8192,3,512]{2,0,1:T(8,128)(2,1)} %param.9) | data formatting | bytes 50331648 | tf_op args[2]
  95.1 0.0 copy-done.2
  95.1 2.9 tile.4
  98.0 67.1 %copy.18 = bf16[4,8,512,640]{3,1,2,0:T(8,128)(2,1)S(1)} copy(bf16[4,8,512,640]{3,2,1,0:T(8,128)(2,1)S(1)} %bitcast.39) | data formatting | bytes 41943040
  165.1 8.1 %slice.42 = bf16[32,327168]{1,0:T(8,128)(2,1)} slice(bf16[32,327680]{1,0:T(8,128)(2,1)S(1)} %bitcast.40), slice={[0:32], [0:327168]} | slice | bytes 41877504 | tf_op jit(solution)/shard_map/slice | solution.py:18
  173.2 0.0 copy-start.1
  173.2 69.0 %reshape.30 = bf16[32,512,639]{2,1,0:T(8,128)(2,1)} reshape(bf16[32,327168]{1,0:T(8,128)(2,1)} %slice.42) | data formatting | bytes 41877504 | tf_op jit(solution)/shard_map/reshape | solution.py:19
  242.2 0.0 copy-done.1
  242.3 0.0 all-gather.3.cloned.1.call-done
  242.3 19.6 %fusion = f32[512,3,512]{2,0,1:T(8,128)S(1)} fusion(bf16[8192,3,512]{0,2,1:T(8,128)(2,1)} %copy.13, bf16[512,8192]{1,0:T(8,128)(2,1)} %all-gather.3.cloned.1.call-done), kind=kOutput, calls=%fused_computation | convolution fusion | flops 12884901888 | bytes 36700160 | tf_op jit(solution)/shard_map/dot_general | solution.py:32
  261.9 0.9 fusion.7
  262.8 0.9 fusion.15
  263.8 2.1 copy.14
  265.9 0.0 copy-start.3
  265.9 9.2 %fusion.2 = f32[32,16,512]{2,1,0:T(8,128)} fusion(bf16[512,32,16]{0,2,1:T(8,128)(2,1)} %bitcast.44, bf16[32,512,639]{2,1,0:T(8,128)(2,1)} %reshape.30), kind=kOutput, calls=%fused_computation.2 | convolution fusion | flops 268435456 | bytes 18350080 | tf_op jit(solution)/shard_map/fst,sfg->tfg/dot_general | solution.py:45
  275.1 2.6 copy.15
  277.6 0.0 copy-done.3
  277.7 2.5 fusion.14
  280.2 0.0 all-gather.5.cloned.1.call-update
  280.2 0.0 all-to-all-done
  280.2 0.0 copy-start
  280.2 12.4 %copy.17 = bf16[16,512,512]{2,1,0:T(8,128)(2,1)} copy(bf16[16,512,512]{1,2,0:T(8,128)(2,1)} %bitcast.15) | data formatting | bytes 16777216 | tf_op jit(solution)/shard_map/all_to_all | solution.py:48
  292.6 71.8 %all-gather.5.cloned.1.call-done = bf16[512,8192]{1,0:T(8,128)(2,1)} async-done(((bf16[512,512]{1,0:T(8,128)(2,1)}), bf16[512,8192]{1,0:T(8,128)(2,1)}) %all-gather.5.cloned.1.call-update) | async-done | bytes 8388624 | tf_op jit(solution)/shard_map/all_gather | solution.py:51
  364.4 0.0 copy-done
  364.4 11.0 %fusion.9 = bf16[512,512]{1,0:T(8,128)(2,1)} fusion(bf16[512,8192]{1,0:T(8,128)(2,1)} %all-gather.5.cloned.1.call-done, bf16[8192,512]{1,0:T(8,128)(2,1)} %bitcast.43, bf16[512,512]{1,0:T(8,128)(2,1)S(1)} %copy-done), kind=kOutput, calls=%fused_computation.14 | convolution fusion | flops 4295753728 | bytes 17825792 | tf_op jit(solution)/shard_map/dot_general | solution.py:50
  (3 shorter events, 0.0 us)
Async XLA Ops:
  6.5 235.7 %all-gather.3.cloned.1.call-start = ((), (), s32[]{:S(2)}) async-start(), calls=%async_computation.1 | async-start | bytes 8912896 | tf_op jit(solution)/shard_map/all_gather | solution.py:33
  56.8 223.4 %all-to-all-start = ((bf16[512,16,512]{0,2,1:T(8,128)(2,1)}), bf16[512,16,512]{0,2,1:T(8,128)(2,1)}, u32[]{:S(2)}, u32[]{:S(2)}) async-start(bf16[512,16,512]{0,2,1:T(8,128)(2,1)} %bitcast.41), calls=%async_computation | async-start | bytes 16777216 | tf_op jit(solution)/shard_map/all_to_all | solution.py:48
  61.6 33.5 %copy-start.2 = (bf16[32,128]{1,0:T(8,128)(2,1)S(1)}, bf16[32,128]{1,0:T(8,128)(2,1)}, u32[]{:S(2)}) copy-start(bf16[32,128]{1,0:T(8,128)(2,1)} %param.11) | copy-start | bytes 24580
  61.6 302.8 %all-gather.5.cloned.1.call-start = ((), (), s32[]{:S(2)}) async-start(), calls=%async_computation.2 | async-start | bytes 8912896 | tf_op jit(solution)/shard_map/all_gather | solution.py:51
  173.2 69.0 %copy-start.1 = (f32[3,3,512]{2,1,0:T(4,128)S(1)}, f32[3,3,512]{2,1,0:T(4,128)}, u32[]{:S(2)}) copy-start(f32[3,3,512]{2,1,0:T(4,128)} %param.10) | copy-start | bytes 55300
  265.9 11.8 %copy-start.3 = (f32[512]{0:T(512)S(1)}, f32[512]{0:T(512)}, u32[]{:S(2)}) copy-start(f32[512]{0:T(512)} %param.12) | copy-start | bytes 6148
  280.2 84.2 %copy-start = (bf16[512,512]{1,0:T(8,128)(2,1)S(1)}, bf16[512,512]{1,0:T(8,128)(2,1)}, u32[]{:S(2)}) copy-start(bf16[512,512]{1,0:T(8,128)(2,1)} %param.7) | copy-start | bytes 1572868
Sparse Core Ops, SparseCore 0:
  44.9 189.7 all-gather.2
  280.3 84.0 all-gather.4
where the time goes:
time: 384 us; the launch traced here: 382 us
  local copies, waits for them, and re-layouts  210 us (55%)
  waiting for transfers between devices  71.8 us (19%)
  matrix products  39.9 us (10%)
  blocking collectives  35 us (9%)
  between operations  13.5 us (4%)
  other arithmetic  7.65 us (2%)
  starting transfers between devices  4.8 us (1%)
    unnamed x11, local copies, waits for them, and re-layouts  113 us
    all_gather x1, waiting for transfers between devices, on_device(): lax.all_gather(hidden, 'tensor', axis=1, tiled=True)  71.8 us
    reshape x1, local copies, waits for them, and re-layouts, lag_matrix(): return tiled.reshape(count, rows, length - 1)[:, :, :rows]  69 us
    psum x1, blocking collectives, on_device(): squares = lax.psum(jnp.sum(wide * wide, axis=1, keepdims=True), 'tensor')  35 us
    dot_general x1, matrix products, on_device(): jnp.dot(lax.all_gather(normed, 'tensor', axis=1, tiled=True), chosen, pre...  19.6 us
    all_to_all x1, local copies, waits for them, and re-layouts, on_device(): lax.all_to_all(w_out, 'tensor', split_axis=1, concat_axis=0, tiled=True)  12.4 us
    dot_general x1, matrix products, on_device(): jnp.dot(lax.all_gather(hidden, 'tensor', axis=1, tiled=True), chosen, pre...  11 us
    dot_general x1, matrix products, on_device(): jnp.einsum('fst,sfg->tfg', lagged, grouped, preferred_element_type=jnp.fl...  9.22 us
  transfers between devices with their start and end apart: 3, of which 1 were waited for; matrix products, arithmetic and copies ran while one was open for 64% of the time, Pallas kernels for 0%

commit v1 on v0

--- a/solution.py
+++ b/solution.py
@@ -20,8 +20,13 @@
 
 
 def on_device(tokens, norm_gain, w_in, w_short, filters, skip, w_out):
+
+    def divide_trees(here_x):
+        top = jnp.sum(jax.lax.all_gather(here_x, axis_name="tensor"), axis=0)
+        return top
+
     wide = tokens.astype(jnp.float32)
-    squares = lax.psum(jnp.sum(wide * wide, axis=1, keepdims=True), "tensor")
+    squares = divide_trees(jnp.sum(wide * wide, axis=1, keepdims=True))
     factor = lax.rsqrt(squares / D + 1e-05)
     normed = (wide * factor * norm_gain[None, :]).astype(jnp.bfloat16)
     width = w_in.shape[0]

time: 384 us -> 372 us (0.969)
  blocking collectives: 35 us -> 23.2 us
    psum x1 -> x0, blocking collectives: 35 us -> none  [on_device(): squares = lax.psum(jnp.sum(wide * wide, axis=1, keepdims=True), 'tensor')]
    all_gather x0 -> x1, blocking collectives: none -> 23.2 us  [divide_trees(): top = jnp.sum(jax.lax.all_gather(here_x, axis_name='tensor'), axis=0)]
  transfers between devices with their start and end apart: 3 -> 3, of which waited for: 1 -> 1; matrix products, arithmetic and copies ran while one was open for 64% -> 66% of each run, Pallas kernels for 0% -> 0%
where the time goes in v1:
time: 372 us; the launch traced here: 371 us
  local copies, waits for them, and re-layouts  210 us (56%)
  waiting for transfers between devices  71.8 us (19%)
  matrix products  39.9 us (11%)
  blocking collectives  23.2 us (6%)
  between operations  13.5 us (4%)
  other arithmetic  7.69 us (2%)
  starting transfers between devices  4.8 us (1%)
    unnamed x11, local copies, waits for them, and re-layouts  113 us
    all_gather x1, waiting for transfers between devices, on_device(): lax.all_gather(hidden, 'tensor', axis=1, tiled=True)  71.8 us
    reshape x1, local copies, waits for them, and re-layouts, lag_matrix(): return tiled.reshape(count, rows, length - 1)[:, :, :rows]  69 us
    all_gather x1, blocking collectives, divide_trees(): top = jnp.sum(jax.lax.all_gather(here_x, axis_name='tensor'), axis=0)  23.2 us
    dot_general x1, matrix products, on_device(): jnp.dot(lax.all_gather(normed, 'tensor', axis=1, tiled=True), chosen, pre...  19.6 us
    all_to_all x1, local copies, waits for them, and re-layouts, on_device(): lax.all_to_all(w_out, 'tensor', split_axis=1, concat_axis=0, tiled=True)  12.4 us
    dot_general x1, matrix products, on_device(): jnp.dot(lax.all_gather(hidden, 'tensor', axis=1, tiled=True), chosen, pre...  11 us
    dot_general x1, matrix products, on_device(): jnp.einsum('fst,sfg->tfg', lagged, grouped, preferred_element_type=jnp.fl...  9.22 us
  transfers between devices with their start and end apart: 3, of which 1 were waited for; matrix products, arithmetic and copies ran while one was open for 66% of the time, Pallas kernels for 0%

profile of v1, /device:TPU:0, one launch (start us, length us, event | category | flops | bytes accessed | tf_op | source)
XLA Modules:
  0.0 370.6 jit_solution(11407496775047296741)
XLA Ops:
  6.5 0.0 all-gather.5.cloned.1.call-start
  6.5 1.2 fusion.10
  7.8 23.2 %all-gather.1 = f32[16,1,512]{2,1,0:T(1,128)S(1)} all-gather(f32[1,1,512]{2,1,0:T(1,128)S(1)} %bitcast.44), channel_id=2, replica_groups=mesh['groups'=2,'tensor'=16] {'tensor'}, dimensions={0}, use_global_device_ids=true | all-gather | bytes 34816 | tf_op jit(solution)/shard_map/all_gather | solution.py:25
  31.0 2.0 fusion.12
  33.0 0.0 all-gather.5.cloned.1.call-update
  33.1 12.1 %copy.21 = bf16[512,8192]{0,1:T(8,128)(2,1)} copy(bf16[512,8192]{1,0:T(8,128)(2,1)} %param.13) | data formatting | bytes 16777216 | tf_op args[6]
  45.1 4.8 %all-to-all-start = ((bf16[512,16,512]{0,2,1:T(8,128)(2,1)}), bf16[512,16,512]{0,2,1:T(8,128)(2,1)}, u32[]{:S(2)}, u32[]{:S(2)}) async-start(bf16[512,16,512]{0,2,1:T(8,128)(2,1)} %bitcast.40), calls=%async_computation | async-start | bytes 16777216 | tf_op jit(solution)/shard_map/all_to_all | solution.py:53
  49.9 0.0 copy-start.2
  49.9 0.0 all-gather.7.cloned.1.call-start
  49.9 33.5 %copy.18 = bf16[8192,3,512]{0,2,1:T(8,128)(2,1)} copy(bf16[8192,3,512]{2,0,1:T(8,128)(2,1)} %param.9) | data formatting | bytes 50331648 | tf_op args[2]
  83.4 0.0 copy-done.2
  83.4 2.9 tile.4
  86.3 67.1 %copy.23 = bf16[4,8,512,640]{3,1,2,0:T(8,128)(2,1)S(1)} copy(bf16[4,8,512,640]{3,2,1,0:T(8,128)(2,1)S(1)} %bitcast.38) | data formatting | bytes 41943040
  153.4 8.1 %slice.42 = bf16[32,327168]{1,0:T(8,128)(2,1)} slice(bf16[32,327680]{1,0:T(8,128)(2,1)S(1)} %bitcast.39), slice={[0:32], [0:327168]} | slice | bytes 41877504 | tf_op jit(solution)/shard_map/slice | solution.py:18
  161.5 0.0 copy-start.1
  161.5 69.0 %reshape.39 = bf16[32,512,639]{2,1,0:T(8,128)(2,1)} reshape(bf16[32,327168]{1,0:T(8,128)(2,1)} %slice.42) | data formatting | bytes 41877504 | tf_op jit(solution)/shard_map/reshape | solution.py:19
  230.5 0.0 copy-done.1
  230.5 0.0 all-gather.5.cloned.1.call-done
  230.6 19.6 %fusion = f32[512,3,512]{2,0,1:T(8,128)S(1)} fusion(bf16[8192,3,512]{0,2,1:T(8,128)(2,1)} %copy.18, bf16[512,8192]{1,0:T(8,128)(2,1)} %all-gather.5.cloned.1.call-done), kind=kOutput, calls=%fused_computation | convolution fusion | flops 12884901888 | bytes 36700160 | tf_op jit(solution)/shard_map/dot_general | solution.py:37
  250.2 0.9 fusion.7
  251.1 0.9 fusion.15
  252.1 2.1 copy.19
  254.1 0.0 copy-start.3
  254.1 9.2 %fusion.2 = f32[32,16,512]{2,1,0:T(8,128)} fusion(bf16[512,32,16]{0,2,1:T(8,128)(2,1)} %bitcast.43, bf16[32,512,639]{2,1,0:T(8,128)(2,1)} %reshape.39), kind=kOutput, calls=%fused_computation.2 | convolution fusion | flops 268435456 | bytes 18350080 | tf_op jit(solution)/shard_map/fst,sfg->tfg/dot_general | solution.py:50
  263.4 2.6 copy.20
  265.9 0.0 copy-done.3
  265.9 2.5 fusion.14
  268.5 0.0 all-gather.7.cloned.1.call-update
  268.5 0.0 all-to-all-done
  268.5 0.0 copy-start
  268.5 12.4 %copy.22 = bf16[16,512,512]{2,1,0:T(8,128)(2,1)} copy(bf16[16,512,512]{1,2,0:T(8,128)(2,1)} %bitcast.14) | data formatting | bytes 16777216 | tf_op jit(solution)/shard_map/all_to_all | solution.py:53
  280.9 71.8 %all-gather.7.cloned.1.call-done = bf16[512,8192]{1,0:T(8,128)(2,1)} async-done(((bf16[512,512]{1,0:T(8,128)(2,1)}), bf16[512,8192]{1,0:T(8,128)(2,1)}) %all-gather.7.cloned.1.call-update) | async-done | bytes 8388624 | tf_op jit(solution)/shard_map/all_gather | solution.py:56
  352.7 0.0 copy-done
  352.7 11.0 %fusion.9 = bf16[512,512]{1,0:T(8,128)(2,1)} fusion(bf16[512,8192]{1,0:T(8,128)(2,1)} %all-gather.7.cloned.1.call-done, bf16[8192,512]{1,0:T(8,128)(2,1)} %bitcast.42, bf16[512,512]{1,0:T(8,128)(2,1)S(1)} %copy-done), kind=kOutput, calls=%fused_computation.14 | convolution fusion | flops 4295753728 | bytes 17825792 | tf_op jit(solution)/shard_map/dot_general | solution.py:55
  (4 shorter events, 0.1 us)
Async XLA Ops:
  6.5 224.0 %all-gather.5.cloned.1.call-start = ((), (), s32[]{:S(2)}) async-start(), calls=%async_computation.1 | async-start | bytes 8912896 | tf_op jit(solution)/shard_map/all_gather | solution.py:38
  45.1 223.4 %all-to-all-start = ((bf16[512,16,512]{0,2,1:T(8,128)(2,1)}), bf16[512,16,512]{0,2,1:T(8,128)(2,1)}, u32[]{:S(2)}, u32[]{:S(2)}) async-start(bf16[512,16,512]{0,2,1:T(8,128)(2,1)} %bitcast.40), calls=%async_computation | async-start | bytes 16777216 | tf_op jit(solution)/shard_map/all_to_all | solution.py:53
  49.9 33.5 %copy-start.2 = (bf16[32,128]{1,0:T(8,128)(2,1)S(1)}, bf16[32,128]{1,0:T(8,128)(2,1)}, u32[]{:S(2)}) copy-start(bf16[32,128]{1,0:T(8,128)(2,1)} %param.11) | copy-start | bytes 24580
  49.9 302.8 %all-gather.7.cloned.1.call-start = ((), (), s32[]{:S(2)}) async-start(), calls=%async_computation.2 | async-start | bytes 8912896 | tf_op jit(solution)/shard_map/all_gather | solution.py:56
  161.5 69.0 %copy-start.1 = (f32[3,3,512]{2,1,0:T(4,128)S(1)}, f32[3,3,512]{2,1,0:T(4,128)}, u32[]{:S(2)}) copy-start(f32[3,3,512]{2,1,0:T(4,128)} %param.10) | copy-start | bytes 55300
  254.1 11.8 %copy-start.3 = (f32[512]{0:T(512)S(1)}, f32[512]{0:T(512)}, u32[]{:S(2)}) copy-start(f32[512]{0:T(512)} %param.12) | copy-start | bytes 6148
  268.5 84.2 %copy-start = (bf16[512,512]{1,0:T(8,128)(2,1)S(1)}, bf16[512,512]{1,0:T(8,128)(2,1)}, u32[]{:S(2)}) copy-start(bf16[512,512]{1,0:T(8,128)(2,1)} %param.7) | copy-start | bytes 1572868
Sparse Core Ops, SparseCore 0:
  33.2 189.7 all-gather.4
  268.6 84.0 all-gather.6
